TPU v7x, 128 devices: a whole 4x4x4 slice. The times are simulated.
128 devices in a mesh: row: 8 (over y_lo, z), col: 16 (over x, y_hi, core).
Axes of the slice: x: 4, y: 4 (y_hi: 2, y_lo: 2; y = y_hi * 2 + y_lo), z: 4, core: 2. Of those that a mesh axis runs over, the one named last changes fastest.
Arguments:
- base_flat: bfloat16 [2, 29568, 8192], P(None, ('row', 'col')), may hold values from -6 to 6
- adjusted_flat: bfloat16 [2, 29568, 8192], P(None, ('row', 'col')), may hold values from -6 to 6
- omega: bfloat16 [2, 8192, 256], P(None, 'col'), may hold values from -6 to 6
Outputs:
- adapter_up_basis: float32 [2, 29568, 256], P(None, ('row', 'col'))
- adapter_down_transposed: float32 [2, 8192, 256], P(None, 'col', 'row')
All inputs are finite; a program needn't handle non-finite values.
Results may differ from a plain program's by a relative error of at most 0.011.
Values may be sent and summed in bfloat16 or wider, within the bound.
A program may use at most 128 MiB of HBM per device.

v0:
```python
import math

import jax
import jax.numpy as jnp
from jax import lax
from jax.sharding import PartitionSpec as P

HIDDEN_UNITS = 29568


def sketch_term(blocks, right):
    terms = []
    for index in range(blocks.shape[0]):
        rows = blocks[index]
        terms.append(jnp.dot(rows, right[index], preferred_element_type=jnp.float32))
    return jnp.concatenate(terms, axis=1)


def gram_of(panel, matrix_list, adapter_rank):
    panel_three = panel.reshape(panel.shape[0], matrix_list, adapter_rank)
    return jnp.einsum("rmk,rml->mkl", panel_three, panel_three, precision=lax.Precision.HIGHEST)


def orthonormal(panel, gram_total, matrix_list, adapter_rank):
    lower = jnp.linalg.cholesky(gram_total)
    stacked = panel.reshape(panel.shape[0], matrix_list, adapter_rank).transpose(1, 2, 0)
    solved = jax.scipy.linalg.solve_triangular(lower, stacked, lower=True)
    return solved.transpose(2, 0, 1).reshape(panel.shape[0], matrix_list * adapter_rank)


def contract(total, blocks, piece):
    adapter_rank = total.shape[2]
    terms = []
    for index in range(blocks.shape[0]):
        rows = blocks[index]
        terms.append(
            lax.dot_general(
                rows,
                piece[:, index * adapter_rank : (index + 1) * adapter_rank],
                (((0,), (0,)), ((), ())),
                preferred_element_type=jnp.float32,
            )
        )
    return jnp.stack(terms)


def local(base_flat, adjusted_flat, omega):
    matrix_list = base_flat.shape[0]
    adapter_rank = omega.shape[2]
    moved_base, moved_adjusted = (
        lax.all_to_all(base_flat, "col", split_axis=2, concat_axis=1, tiled=True),
        lax.all_to_all(adjusted_flat, "col", split_axis=2, concat_axis=1, tiled=True),
    )
    blocks = (moved_adjusted.astype(jnp.float32) - moved_base.astype(jnp.float32)).astype(
        jnp.bfloat16
    )
    block_rows = blocks.shape[1]
    block_cols = blocks.shape[2]
    segment_rows = block_rows // lax.axis_size("col")
    col_index = lax.axis_index("col")
    empty = jnp.zeros((matrix_list, block_cols, adapter_rank), jnp.float32)

    def find_basis(right):
        panel = lax.psum(sketch_term(blocks, right), "col")
        gram_total = lax.psum(gram_of(panel, matrix_list, adapter_rank), "row")
        basis = orthonormal(panel, gram_total, matrix_list, adapter_rank)
        own_rows = lax.dynamic_slice_in_dim(basis, col_index * segment_rows, segment_rows, 0)
        folded = contract(empty, blocks, basis.astype(jnp.bfloat16))
        return (own_rows, folded)

    first_rows, first_folded = find_basis(omega)
    shares = lax.psum_scatter(first_folded, "row", scatter_dimension=1, tiled=True)
    columns = lax.all_gather(shares.astype(jnp.bfloat16), "row", axis=1, tiled=True)
    last_basis_rows, last_folded_rows = find_basis(columns)
    adapter_down_transposed = lax.psum_scatter(
        last_folded_rows.astype(jnp.bfloat16), "row", scatter_dimension=2, tiled=True
    ).astype(jnp.float32)
    adapter_up_basis = (
        (math.sqrt(HIDDEN_UNITS) * last_basis_rows)
        .reshape(segment_rows, matrix_list, adapter_rank)
        .transpose(1, 0, 2)
    )
    return (adapter_up_basis, adapter_down_transposed)


def solution(mesh):
    in_specs = (P(None, ("row", "col"), None), P(None, ("row", "col"), None), P(None, "col", None))
    out_specs = (P(None, ("row", "col"), None), P(None, "col", "row"))
    return jax.shard_map(local, mesh=mesh, in_specs=in_specs, out_specs=out_specs, check_vma=False)
```

profile of v0, /device:TPU:0, one launch (start us, length us, event | category | flops | bytes accessed | tf_op | source)
XLA Modules:
  0.0 1382.9 jit_solution(16031709990413155356)
XLA Ops:
  7.2 28.5 %copy.91 = bf16[2,231,8192]{1,0,2:T(2,128)(2,1)} copy(bf16[2,231,8192]{2,0,1:T(2,128)(2,1)} %param.7) | data formatting | bytes 15138816 | tf_op args[1]
  35.7 7.2 all-to-all-start
  42.9 28.4 %copy.92 = bf16[2,231,8192]{1,0,2:T(2,128)(2,1)} copy(bf16[2,231,8192]{2,0,1:T(2,128)(2,1)} %param.6) | data formatting | bytes 15138816 | tf_op args[0]
  71.3 103.6 %all-to-all-done = bf16[2,231,8192]{1,0,2:T(2,128)(2,1)} async-done(((bf16[2,231,8192]{1,0,2:T(2,128)(2,1)}), bf16[2,231,8192]{1,0,2:T(2,128)(2,1)}, u32[]{:S(2)}, u32[]{:S(2)}) %all-to-all-start) | async-done | bytes 7569440 | tf_op jit(solution)/shard_map/all_to_all | solution.py:52
  174.9 105.0 %all_to_all.8 = bf16[2,231,8192]{1,0,2:T(2,128)(2,1)S(1)} all-to-all(bf16[2,231,8192]{1,0,2:T(2,128)(2,1)} %copy.92), channel_id=1, replica_groups=mesh['row'=8,'col'=16] {'col'}, dimensions={2} | all-to-all | bytes 15138816 | tf_op jit(solution)/shard_map/all_to_all | solution.py:51
  279.9 10.9 subtract_convert_fusion
  290.8 20.9 %copy.93 = bf16[2,231,16,512]{3,1,2,0:T(8,128)(2,1)} copy(bf16[2,231,16,512]{1,0,3,2:T(2,128)(2,1)} %bitcast.134) | data formatting | bytes 15138816 | tf_op jit(solution)/shard_map/sub | solution.py:54
  311.7 5.4 fusion.53
  317.1 3.9 squeeze.26
  321.0 4.0 squeeze.24
  325.1 3.4 fusion.35
  330.8 3.7 copy.138
  334.7 184.1 %all-reduce.8.cloned.1.call-done = f32[3696,2,256]{2,0,1:T(8,128)} async-done(((f32[3696,2,256]{2,0,1:T(8,128)}), f32[3696,2,256]{2,0,1:T(8,128)}) %all-reduce.8.cloned.1.call-update) | async-done | bytes 7569424 | tf_op jit(solution)/shard_map/psum | solution.py:64
  518.8 18.3 %fusion.54 = f32[2,256,256]{1,2,0:T(8,128)} fusion(f32[3696,2,256]{2,0,1:T(8,128)} %all-reduce.8.cloned.1.call-done), kind=kOutput, calls=%fused_computation.90 | convolution fusion | flops 5813305344 | bytes 8093696 | tf_op jit(solution)/shard_map/rmk,rml->mkl/dot_general | solution.py:21
  538.1 74.6 %all-reduce.10.cloned.1.call-done = f32[2,256,256]{1,2,0:T(8,128)} async-done(((f32[2,256,256]{1,2,0:T(8,128)}), f32[2,256,256]{1,2,0:T(8,128)}) %all-reduce.10.cloned.1.call-update) | async-done | bytes 524304 | tf_op jit(solution)/shard_map/psum | solution.py:65
  612.7 2.1 copy.96
  614.8 1.4 fusion.32
  617.6 24.3 %custom-call.17 = f32[2,128,128]{2,1,0:T(8,128)S(1)} custom-call(f32[2,128,128]{2,1,0:T(8,128)} %cholesky.198), custom_call_target="Cholesky" | custom-call | tf_op jit(solution)/shard_map/jit(cholesky)/cholesky | solution.py:25
  642.6 21.1 %custom-call.18 = f32[2,1,128,128]{2,3,1,0:T(8,128)} custom-call(f32[2,1,128,128]{3,2,1,0:T(8,128)} %select_bitcast_fusion.1), custom_call_target="InvertDiagBlocksLowerTriangular" | custom-call | tf_op jit(solution)/shard_map/jit(cholesky)/cholesky | solution.py:25
  664.6 1.9 constant_dynamic-update-slice_fusion.3
  666.5 2.0 convolution_subtract_fusion.3
  668.4 24.9 %custom-call.19 = f32[2,128,128]{2,1,0:T(8,128)} custom-call(f32[2,128,128]{2,1,0:T(8,128)} %convolution_subtract_fusion.3), custom_call_target="Cholesky" | custom-call | tf_op jit(solution)/shard_map/jit(cholesky)/cholesky | solution.py:25
  693.3 1.6 select_reduce_fusion.2
  695.1 2.0 select_select_fusion.1
  697.9 7.0 while.4
  698.5 2.9 bitcast_dynamic-update-slice_fusion.4
  702.0 2.9 bitcast_dynamic-update-slice_fusion.4
  704.9 41.2 %custom-call.20 = f32[2,2,128,128]{2,3,1,0:T(8,128)} custom-call(f32[2,2,128,128]{3,2,1,0:T(8,128)} %bitcast.146), custom_call_target="InvertDiagBlocksLowerTriangular" | custom-call | tf_op jit(solution)/shard_map/jit(_solve_triangular)/vmap()/triangular_solve | solution.py:27
  746.1 5.9 fusion.3
  752.0 4.7 convolution_subtract_fusion.1
  756.8 3.5 fusion.46
  760.3 2.5 fusion
  762.8 6.2 copy.102
  769.0 4.0 fusion.13
  776.3 38.8 %reduce-scatter.2.cloned.1.call-done = f32[2,64,256]{2,1,0:T(8,128)} async-done(((f32[2,512,256]{2,1,0:T(8,128)}), f32[2,64,256]{2,1,0:T(8,128)}) %reduce-scatter.2.cloned.1.call-update) | async-done | bytes 131088 | tf_op jit(solution)/shard_map/reduce_scatter | solution.py:72
  816.0 29.0 %all_gather.3 = bf16[2,512,256]{2,1,0:T(8,128)(2,1)S(1)} all-gather(bf16[2,64,256]{2,1,0:T(8,128)(2,1)S(1)} %convert_element_type.42), channel_id=1, replica_groups=mesh['row'=8,'col'=16] {'row'}, dimensions={1}, use_global_device_ids=true | all-gather | bytes 589824 | tf_op jit(solution)/shard_map/all_gather | solution.py:73
  845.0 3.4 fusion.34
  850.7 3.7 copy.137
  854.5 183.3 %all-reduce.12.cloned.1.call-done = f32[3696,2,256]{2,0,1:T(8,128)} async-done(((f32[3696,2,256]{2,0,1:T(8,128)}), f32[3696,2,256]{2,0,1:T(8,128)}) %all-reduce.12.cloned.1.call-update) | async-done | bytes 7569424 | tf_op jit(solution)/shard_map/psum | solution.py:64
  1037.8 18.3 %fusion.55 = f32[2,256,256]{1,2,0:T(8,128)} fusion(f32[3696,2,256]{2,0,1:T(8,128)} %all-reduce.12.cloned.1.call-done), kind=kOutput, calls=%fused_computation.91 | convolution fusion | flops 5813305344 | bytes 8093696 | tf_op jit(solution)/shard_map/rmk,rml->mkl/dot_general | solution.py:21
  1056.2 75.5 %all-reduce.14.cloned.1.call-done = f32[2,256,256]{1,2,0:T(8,128)} async-done(((f32[2,256,256]{1,2,0:T(8,128)}), f32[2,256,256]{1,2,0:T(8,128)}) %all-reduce.14.cloned.1.call-update) | async-done | bytes 524304 | tf_op jit(solution)/shard_map/psum | solution.py:65
  1131.7 2.1 copy.105
  1133.8 1.4 fusion.31
  1136.6 24.6 %custom-call.21 = f32[2,128,128]{2,1,0:T(8,128)S(1)} custom-call(f32[2,128,128]{2,1,0:T(8,128)} %cholesky.201), custom_call_target="Cholesky" | custom-call | tf_op jit(solution)/shard_map/jit(cholesky)/cholesky | solution.py:25
  1162.8 21.1 %custom-call.22 = f32[2,1,128,128]{2,3,1,0:T(8,128)} custom-call(f32[2,1,128,128]{3,2,1,0:T(8,128)} %select_bitcast_fusion), custom_call_target="InvertDiagBlocksLowerTriangular" | custom-call | tf_op jit(solution)/shard_map/jit(cholesky)/cholesky | solution.py:25
  1183.9 1.9 constant_dynamic-update-slice_fusion.1
  1185.9 1.9 convolution_subtract_fusion.2
  1187.8 24.9 %custom-call.23 = f32[2,128,128]{2,1,0:T(8,128)} custom-call(f32[2,128,128]{2,1,0:T(8,128)} %convolution_subtract_fusion.2), custom_call_target="Cholesky" | custom-call | tf_op jit(solution)/shard_map/jit(cholesky)/cholesky | solution.py:25
  1212.7 1.6 select_reduce_fusion
  1214.6 2.0 select_select_fusion
  1217.3 7.0 while.5
  1217.9 2.9 bitcast_dynamic-update-slice_fusion.5
  1221.4 2.9 bitcast_dynamic-update-slice_fusion.5
  1224.3 40.9 %custom-call.24 = f32[2,2,128,128]{2,3,1,0:T(8,128)} custom-call(f32[2,2,128,128]{3,2,1,0:T(8,128)} %bitcast.145), custom_call_target="InvertDiagBlocksLowerTriangular" | custom-call | tf_op jit(solution)/shard_map/jit(_solve_triangular)/vmap()/triangular_solve | solution.py:27
  1265.2 5.5 fusion.1
  1270.7 4.2 convolution_subtract_fusion
  1274.9 3.3 fusion.42
  1278.2 3.6 maximum_bitcast_fusion
  1281.8 8.9 copy.111
  1290.7 3.7 bitcast_convert_fusion
  1295.0 1.2 fusion.28
  1297.0 1.2 fusion.25
  1300.8 1.3 dynamic-slice_multiply_fusion
  1303.1 71.1 %all-reduce.16.cloned.1.call-done = bf16[2,512,256]{1,0,2:T(2,128)(2,1)} async-done(((bf16[2,512,256]{1,0,2:T(2,128)(2,1)}), bf16[2,512,256]{1,0,2:T(2,128)(2,1)}) %all-reduce.16.cloned.1.call-update) | async-done | bytes 524304
  (85 shorter events, 26.2 us)
Async XLA Ops:
  35.7 139.2 %all-to-all-start = ((bf16[2,231,8192]{1,0,2:T(2,128)(2,1)}), bf16[2,231,8192]{1,0,2:T(2,128)(2,1)}, u32[]{:S(2)}, u32[]{:S(2)}) async-start(bf16[2,231,8192]{1,0,2:T(2,128)(2,1)} %copy.91), calls=%async_computation | async-start | bytes 16777216 | tf_op jit(solution)/shard_map/all_to_all | solution.py:52
  42.8 475.9 %all-reduce.8.cloned.1.call-start = ((), (), s32[]{:S(2)}) async-start(), calls=%async_computation.3 | async-start | bytes 15138816 | tf_op jit(solution)/shard_map/psum | solution.py:64
  321.0 4.0 copy-start.8
  325.1 3.4 copy-start.3
  334.5 278.2 %all-reduce.10.cloned.1.call-start = ((), (), s32[]{:S(2)}) async-start(), calls=%async_computation.4 | async-start | bytes 1048576 | tf_op jit(solution)/shard_map/psum | solution.py:65
  537.1 278.0 %reduce-scatter.2.cloned.1.call-start = ((), (), s32[]{:S(2)}) async-start(), calls=%async_computation.5 | async-start | bytes 1179648 | tf_op jit(solution)/shard_map/reduce_scatter | solution.py:72
  614.8 137.2 %slice-start = ((s8[7569408]{0:T(1024)(128)(4,1)}), s8[3375104]{0:T(1024)(128)(4,1)S(1)}, s32[]{:S(2)}) async-start(s8[7569408]{0:T(1024)(128)(4,1)} %bitcast.127), calls=%async_computation.9 | async-start | bytes 6750208
  616.2 0.8 copy-start.7
  746.1 5.9 slice-start.1
  752.0 4.8 copy-start.10
  769.0 4.1 copy-start
  769.0 4.9 copy-start.5
  776.2 261.6 %all-reduce.12.cloned.1.call-start = ((), (), s32[]{:S(2)}) async-start(), calls=%async_computation.6 | async-start | bytes 15138816 | tf_op jit(solution)/shard_map/psum | solution.py:64
  845.0 3.4 copy-start.1
  854.4 277.3 %all-reduce.14.cloned.1.call-start = ((), (), s32[]{:S(2)}) async-start(), calls=%async_computation.7 | async-start | bytes 1048576 | tf_op jit(solution)/shard_map/psum | solution.py:65
  1056.1 318.1 %all-reduce.16.cloned.1.call-start = ((), (), s32[]{:S(2)}) async-start(), calls=%async_computation.8 | async-start | bytes 1048576
  1133.8 136.9 %slice-start.2 = ((s8[7569408]{0:T(1024)(128)(4,1)}), s8[3375104]{0:T(1024)(128)(4,1)S(1)}, s32[]{:S(2)}) async-start(s8[7569408]{0:T(1024)(128)(4,1)} %bitcast.131), calls=%async_computation.11 | async-start | bytes 6750208
  1135.2 0.8 copy-start.6
  1265.2 5.5 slice-start.3
  1270.7 4.2 copy-start.9
  1290.7 4.2 copy-start.4
  1295.0 2.1 copy-start.2
  1297.0 2.5 copy-start.11
Sparse Core Ops, SparseCore 0:
  334.6 184.1 all-reduce.7
  537.2 75.4 all-reduce.9
  776.3 38.6 reduce-scatter.1
  854.5 183.2 all-reduce.11
  1056.2 75.3 all-reduce.13
  1299.7 74.4 all-reduce.15
where the time goes:
time: 1390 us; the launch traced here: 1380 us
  waiting for transfers between devices  731 us (53%)
  other arithmetic  263 us (19%)
  local copies, waits for them, and re-layouts  144 us (10%)
  blocking collectives  134 us (10%)
  matrix products  88.2 us (6%)
  between operations  15.4 us (1%)
    psum x2, waiting for transfers between devices, find_basis(): panel = lax.psum(sketch_term(blocks, right), 'col')  367 us
    psum x2, waiting for transfers between devices, find_basis(): gram_total = lax.psum(gram_of(panel, matrix_list, adapter_rank), 'row')  150 us
    another operation x17, other arithmetic, orthonormal(): lower = jnp.linalg.cholesky(gram_total)  146 us
    all_to_all x1, blocking collectives, local(): lax.all_to_all(base_flat, 'col', split_axis=2, concat_axis=1, tiled=True)  105 us
    all_to_all x1, waiting for transfers between devices, local(): lax.all_to_all(adjusted_flat, 'col', split_axis=2, concat_axis=1, tiled=T...  104 us
    another operation x6, other arithmetic, orthonormal(): solved = jax.scipy.linalg.solve_triangular(lower, stacked, lower=True)  86.7 us
    unnamed x7, waiting for transfers between devices  71.2 us
    unnamed x36, local copies, waits for them, and re-layouts  62 us
  transfers between devices with their start and end apart: 7, of which 7 were waited for; matrix products, arithmetic and copies ran while one was open for 2% of the time, Pallas kernels for 0%

commit v1 on v0

v1 whole, which is shorter than its diff:
```python
import math

import jax
import jax.numpy as jnp
from jax import lax
from jax.experimental import pallas as pl
from jax.experimental.pallas import tpu as pltpu
from jax.sharding import PartitionSpec as P

HI = lax.Precision.HIGHEST
MESH = pl.DeviceIdType.MESH
NB = 16
ROWS, PAD, WIDE, RANK, SUB = 231, 240, 512, 256, 128
ORDERS = ((0, 1, 2), (1, 2, 0), (2, 0, 1))
CUT_RS = ((0, 96), (96, 80), (176, 80))
CUT_AG = ((0, 48), (48, 48), (96, 32))


def dot(a, b, ca, cb, precision=None):
    return lax.dot_general(a, b, (((ca,), (cb,)), ((), ())), precision=precision, preferred_element_type=jnp.float32)

def factor_panel(work):
    size = 128
    lane = lax.broadcasted_iota(jnp.int32, (NB, size), 1)
    sub = lax.broadcasted_iota(jnp.int32, (NB, size), 0)
    def step(k, carry):
        start = pl.multiple_of(k * NB, NB)
        rows = work[pl.ds(start, NB), :]
        x = pltpu.roll(rows[:, :size], lax.rem(size - start, size), 1)
        x = jnp.where(lane < NB, x, jnp.where(lane == sub + NB, 1.0, 0.0))
        for j in range(NB - 1):
            inv = 1.0 / x[j : j + 1, j : j + 1]
            mult = x[:, j : j + 1] * inv
            mult = jnp.where(sub > j, jnp.broadcast_to(mult, (NB, size)), 0.0)
            x = x - mult * jnp.broadcast_to(x[j : j + 1, :], (NB, size))
        diag = jnp.sum(jnp.where(lane == sub, x, 0.0), axis=1, keepdims=True)
        t = x[:, NB : 2 * NB] * lax.rsqrt(diag)
        new = dot(t, rows, 1, 0, HI)
        left = jnp.where(lane >= start + NB, new[:, :size], 0.0)
        work[...] -= dot(left, new, 0, 0, HI)
        work[pl.ds(start, NB), :] = new
        return carry
    lax.fori_loop(0, size // NB, step, 0)

def invert_factor(gram, work, out):
    size = 128
    eye = (lax.broadcasted_iota(jnp.int32, (size, size), 0) == lax.broadcasted_iota(jnp.int32, (size, size), 1)).astype(jnp.float32)
    work[:, :size] = gram[0:16].reshape(size, size)
    work[:, size:] = eye
    factor_panel(work)
    t11 = work[:, size:]
    l21 = dot(gram[16:32].reshape(size, size), t11, 1, 1, HI)
    out[:size, :size] = t11
    out[:size, size:] = jnp.zeros((size, size), jnp.float32)
    out[size:, :size] = dot(l21, t11, 1, 0, HI)
    work[:, :size] = gram[48:64].reshape(size, size) - dot(l21, l21, 1, 1, HI)
    work[:, size:] = eye
    factor_panel(work)
    t22 = work[:, size:]
    out[size:, :size] = -dot(t22, out[size:, :size], 1, 0, HI)
    out[size:, size:] = t22


def device_at(pos, core):
    x, y, z = pos
    return {"row": lax.rem(y, 2) * 4 + z, "col": x * 4 + lax.div(y, 2) * 2 + core}


def moved(pos, axis, step):
    return tuple(lax.rem(p + step, 4) if a == axis else p for a, p in enumerate(pos))


def send(src, dst, send_sem, recv_sem, device):
    return pltpu.make_async_remote_copy(
        src_ref=src, dst_ref=dst, send_sem=send_sem, recv_sem=recv_sem, device_id=device, device_id_type=MESH
    )


def reduce_scatter(pos, core, source, bufs, total, send_sems, recv_sems):
    copies = {}

    def launch(part, stage, block):
        axis = ORDERS[part][stage]
        copies[part, stage] = []
        for step in (2, 1, 3):
            to = moved(pos, axis, step)
            copy = send(
                block(to[axis]),
                bufs[part][2 * stage].at[step - 1],
                send_sems.at[part, stage, step - 1],
                recv_sems.at[part, stage, step - 1],
                device_at(to, core),
            )
            copy.start()
            copies[part, stage].append(copy)

    def first(part, at):
        start, size = CUT_RS[part]
        rows = pl.ds(start, size)
        axis = ORDERS[part][0]
        if axis == 0:
            return source.at[at, :, :, rows]
        if axis == 1:
            return source.at[:, at, :, rows]
        return source.at[:, :, at, rows]

    def second(part, at):
        held = bufs[part][1]
        return held.at[:, at] if part == 1 else held.at[at]

    def arrived(part, stage):
        for copy in copies[part, stage]:
            copy.wait_recv()

    for part in range(3):
        launch(part, 0, lambda at, part=part: first(part, at))
    for part in range(3):
        arrived(part, 0)
        here, got, held = first(part, pos[ORDERS[part][0]]), bufs[part][0], bufs[part][1]

        @pl.loop(0, 16)
        def _(n, here=here, got=got, held=held):
            a, b = lax.div(n, 4), lax.rem(n, 4)
            value = here[a, b].astype(jnp.float32)
            for step in range(3):
                value += got[step, a, b].astype(jnp.float32)
            held[a, b] = value.astype(jnp.bfloat16)

        launch(part, 1, lambda at, part=part: second(part, at))
    for part in range(3):
        arrived(part, 1)
        here, got, held = second(part, pos[ORDERS[part][1]]), bufs[part][2], bufs[part][3]
        for a in range(4):
            value = here[a].astype(jnp.float32)
            for step in range(3):
                value += got[step, a].astype(jnp.float32)
            held[a] = value.astype(jnp.bfloat16)
        launch(part, 2, lambda at, held=held: held.at[at])
    for part in range(3):
        arrived(part, 2)
        start, size = CUT_RS[part]
        value = bufs[part][3][pos[ORDERS[part][2]]].astype(jnp.float32)
        for step in range(3):
            value += bufs[part][4][step].astype(jnp.float32)
        total[start : start + size, :] = value
    for part in range(3):
        for stage in range(3):
            for copy in copies[part, stage]:
                copy.wait_send()


def all_gather(pos, core, blocks, send_sems, recv_sems):
    copies = {}

    def launch(part, stage):
        start, size = CUT_AG[part]
        done = ORDERS[part][:stage]
        index = tuple(slice(None) if a in done else pos[a] for a in range(3)) + (pl.ds(start, size),)
        axis = ORDERS[part][stage]
        copies[part, stage] = []
        for step in (2, 1, 3):
            copy = send(
                blocks.at[index],
                blocks.at[index],
                send_sems.at[part, stage, step - 1],
                recv_sems.at[part, stage, step - 1],
                device_at(moved(pos, axis, step), core),
            )
            copy.start()
            copies[part, stage].append(copy)

    for stage in range(3):
        for part in range(3):
            if stage:
                for copy in copies[part, stage - 1]:
                    copy.wait_recv()
            launch(part, stage)
    for part in range(3):
        for copy in copies[part, 2]:
            copy.wait_recv()
    for part in range(3):
        for stage in range(3):
            for copy in copies[part, stage]:
                copy.wait_send()


def gram_sum(pos, core, panel, pieces, got, mine, whole, sems):
    chip = pos[0] * 16 + pos[1] * 4 + pos[2]
    gram = dot(panel, panel, 0, 0, HI)
    pieces[0:32] = gram[:, :SUB].reshape(32, 8, SUB)
    pieces[32:64] = gram[:, SUB:].reshape(32, 8, SUB)

    def peer(step):
        to = lax.rem(chip + step, 64)
        return to, device_at((lax.div(to, 16), lax.rem(lax.div(to, 4), 4), lax.rem(to, 4)), core)

    @pl.loop(1, 64)
    def _(step):
        to, device = peer(step)
        send(pieces.at[to], got.at[step], sems.at[0], sems.at[1], device).start()

    got[0] = pieces[chip]
    everyone = send(pieces.at[pl.ds(1, 63)], got.at[pl.ds(1, 63)], sems.at[0], sems.at[1], peer(1)[1])
    everyone.wait_recv()
    value = jnp.sum(got[...], axis=0)
    mine[...] = value
    whole[chip] = value

    @pl.loop(1, 64)
    def _(step):
        send(mine, whole.at[chip], sems.at[2], sems.at[3], peer(step)[1]).start()

    everyone.wait_send()
    last = send(got.at[pl.ds(1, 63)], whole.at[pl.ds(1, 63)], sems.at[2], sems.at[3], peer(1)[1])
    last.wait_recv()
    last.wait_send()


def kernel(base, adjusted, omega, up, down, *scratch):
    (
        load_base, load_adjusted, load_sems, delta, outgoing, delta_sems, sketch_map, map_sems,
        sketch, sketch_got, power, power_got, swap_sems, turned, source,
        *rest,
    ) = scratch
    bufs = [rest[5 * part : 5 * part + 5] for part in range(3)]
    (
        total, rs_send, rs_recv, columns, ag_send, ag_recv,
        pieces, gram_got, gram_mine, gram, gram_sems, work, factor, spread, spread_send, spread_recv,
    ) = rest[15:]
    row, col = lax.axis_index("row"), lax.axis_index("col")
    core = lax.rem(col, 2)
    pos = (lax.div(col, 4), lax.rem(lax.div(col, 2), 2) * 2 + lax.div(row, 4), lax.rem(row, 4))
    mate = device_at(pos, 1 - core)
    own = lax.div(col, 2)
    chip = pos[0] * 16 + pos[1] * 4 + pos[2]

    def load(n):
        slot = n % 4
        block = 2 * (n % 8) + ((1 - core) if n < 8 else core)
        lanes = pl.ds(pl.multiple_of(block * WIDE, WIDE), WIDE)
        return (
            pltpu.make_async_copy(base.at[:, :, lanes], load_base.at[slot], load_sems.at[slot, 0]),
            pltpu.make_async_copy(adjusted.at[:, :, lanes], load_adjusted.at[slot], load_sems.at[slot, 1]),
        )

    for n in range(4):
        for copy in load(n):
            copy.start()
    own_map = pltpu.make_async_copy(omega, sketch_map.at[own], map_sems.at[14])
    own_map.start()

    barrier = pltpu.get_barrier_semaphore()
    pl.semaphore_signal(barrier, 1, device_id=mate, device_id_type=MESH)

    @pl.loop(1, 64)
    def _(step):
        to = lax.rem(chip + step, 64)
        device = device_at((lax.div(to, 16), lax.rem(lax.div(to, 4), 4), lax.rem(to, 4)), core)
        pl.semaphore_signal(barrier, 1, device_id=device, device_id_type=MESH)

    pl.semaphore_wait(barrier, 64)

    map_copies = []
    for step in range(1, 8):
        far = (lax.rem(pos[0] + step // 2, 4), lax.rem(pos[1] + 2 * (step % 2), 4), pos[2])
        copy = send(omega, sketch_map.at[own], map_sems.at[step - 1], map_sems.at[step + 6], device_at(far, core))
        copy.start()
        map_copies.append(copy)

    delta_copies = []
    zeros = jnp.zeros((2, PAD - 224, WIDE), jnp.bfloat16)
    for n in range(16):
        for copy in load(n):
            copy.wait()
        place = outgoing.at[n] if n < 8 else delta.at[n - 8, core]
        place[:, 224:, :] = zeros
        for m in range(2):
            value = load_adjusted[n % 4, m].astype(jnp.float32) - load_base[n % 4, m].astype(jnp.float32)
            place[m, 0:ROWS, :] = value.astype(jnp.bfloat16)
        if n < 12:
            for copy in load(n + 4):
                copy.start()
        if n < 8:
            copy = send(outgoing.at[n], delta.at[n, core], delta_sems.at[0, n], delta_sems.at[1, n], mate)
            copy.start()
            delta_copies.append(copy)
    own_map.wait()
    for copy in map_copies + delta_copies:
        copy.wait()

    def swap(part, got, which):
        copy = send(part, got, swap_sems.at[0, which], swap_sems.at[1, which], mate)
        copy.start()
        copy.wait()

    def product(right, part):
        for m in range(2):
            part[m] = jnp.zeros((2 * PAD, RANK), jnp.float32)

            @pl.loop(0, 8)
            def _(i, m=m):
                part[m] += dot(delta[i, :, m].reshape(2 * PAD, WIDE), right(i, m), 1, 0)

    def folded():
        for m in range(2):

            @pl.loop(0, 8)
            def _(i, m=m):
                value = dot(turned[m], delta[i, :, m].reshape(2 * PAD, WIDE), 1, 0).astype(jnp.bfloat16)
                for z in range(4):
                    source[lax.div(i, 2), lax.rem(i, 2) * 2 + m, z] = value[:, z * SUB : (z + 1) * SUB]

        reduce_scatter(pos, core, source, bufs, total, rs_send, rs_recv)

    def orthonormal(panel, which):
        gram_sum(pos, core, panel[core], pieces, gram_got, gram_mine, gram, gram_sems)
        invert_factor(gram, work, factor.at[core])
        swap(factor.at[core], factor.at[core], which)
        for m in range(2):
            turned[m] = dot(factor[m], panel[m], 1, 1, HI).astype(jnp.bfloat16)

    product(lambda i, m: sketch_map[i, m], sketch)
    swap(sketch, sketch_got, 0)
    sketch[...] += sketch_got[...]
    orthonormal(sketch, 1)
    folded()
    columns[pos[0], pos[1], pos[2]] = total[...].T.astype(jnp.bfloat16)
    all_gather(pos, core, columns, ag_send, ag_recv)
    product(
        lambda i, m: columns[lax.div(i, 2), lax.rem(i, 2) * 2 + m].reshape(WIDE, RANK),
        power,
    )
    swap(power, power_got, 2)
    power[...] += power_got[...]
    orthonormal(power, 3)
    for m in range(2):
        rows = power[m, pl.ds(pl.multiple_of(core * PAD, PAD), PAD), :]
        up[m] = (dot(rows, factor[m], 1, 1, HI) * math.sqrt(29568))[:ROWS]
    folded()

    spread_copies = []
    for step in range(1, 8):
        to = lax.rem(row + step, 8)
        rows = pl.ds(pl.multiple_of(to * 32, 32), 32)
        copy = send(
            total.at[rows],
            spread.at[row],
            spread_send.at[step - 1],
            spread_recv.at[step - 1],
            {"row": to, "col": col},
        )
        copy.start()
        spread_copies.append(copy)
    spread[row] = total[pl.ds(pl.multiple_of(row * 32, 32), 32), :]
    for copy in spread_copies:
        copy.wait()
    for n in range(8):
        down[n // 4, (n % 4) * SUB : (n % 4 + 1) * SUB, :] = spread[n].T


def scratch_shapes():
    half, full = jnp.bfloat16, jnp.float32
    dma = pltpu.SemaphoreType.DMA
    parts = []
    for _, size in CUT_RS:
        parts += [
            pltpu.VMEM((3, 4, 4, size, SUB), half),
            pltpu.VMEM((4, 4, size, SUB), half),
            pltpu.VMEM((3, 4, size, SUB), half),
            pltpu.VMEM((4, size, SUB), half),
            pltpu.VMEM((3, size, SUB), half),
        ]
    return [
        pltpu.VMEM((4, 2, ROWS, WIDE), half),
        pltpu.VMEM((4, 2, ROWS, WIDE), half),
        dma((4, 2)),
        pltpu.VMEM((8, 2, 2, PAD, WIDE), half),
        pltpu.VMEM((8, 2, PAD, WIDE), half),
        dma((2, 8)),
        pltpu.VMEM((8, 2, WIDE, RANK), half),
        dma((15,)),
        pltpu.VMEM((2, 2 * PAD, RANK), full),
        pltpu.VMEM((2, 2 * PAD, RANK), full),
        pltpu.VMEM((2, 2 * PAD, RANK), full),
        pltpu.VMEM((2, 2 * PAD, RANK), full),
        dma((2, 4)),
        pltpu.VMEM((2, RANK, 2 * PAD), half),
        pltpu.VMEM((4, 4, 4, RANK, SUB), half),
        *parts,
        pltpu.VMEM((RANK, SUB), full),
        dma((3, 3, 3)),
        dma((3, 3, 3)),
        pltpu.VMEM((4, 4, 4, SUB, RANK), half),
        dma((3, 3, 3)),
        dma((3, 3, 3)),
        pltpu.VMEM((64, 8, SUB), full),
        pltpu.VMEM((64, 8, SUB), full),
        pltpu.VMEM((8, SUB), full),
        pltpu.VMEM((64, 8, SUB), full),
        dma((4,)),
        pltpu.VMEM((SUB, 2 * SUB), full),
        pltpu.VMEM((2, RANK, RANK), full),
        pltpu.VMEM((8, 32, SUB), full),
        dma((7,)),
        dma((7,)),
    ]


def local(base_flat, adjusted_flat, omega):
    anywhere = pl.BlockSpec(memory_space=pl.ANY)
    vmem = pl.BlockSpec(memory_space=pltpu.VMEM)
    return pl.pallas_call(
        kernel,
        out_shape=(
            jax.ShapeDtypeStruct((2, ROWS, RANK), jnp.float32),
            jax.ShapeDtypeStruct((2, WIDE, 32), jnp.float32),
        ),
        in_specs=[anywhere] * 3,
        out_specs=(vmem, vmem),
        scratch_shapes=scratch_shapes(),
        compiler_params=pltpu.CompilerParams(
            collective_id=0, has_side_effects=True, vmem_limit_bytes=60 * 2**20
        ),
    )(base_flat, adjusted_flat, omega)


def solution(mesh):
    in_specs = (P(None, ("row", "col"), None), P(None, ("row", "col"), None), P(None, "col", None))
    out_specs = (P(None, ("row", "col"), None), P(None, "col", "row"))
    return jax.shard_map(local, mesh=mesh, in_specs=in_specs, out_specs=out_specs, check_vma=False)
```

time: 1390 us -> 317 us (0.23)
  waiting for transfers between devices: 731 us -> 0 us
  Pallas kernels: 0 us -> 292 us
  other arithmetic: 263 us -> 0 us
  blocking collectives: 134 us -> 0 us
  local copies, waits for them, and re-layouts: 144 us -> 23.9 us
  matrix products: 88.2 us -> 0 us
  between operations: 15.4 us -> 0.65 us
    psum x4 -> x0, waiting for transfers between devices: 518 us -> none  [the longest x2 367 us: find_basis(): panel = lax.psum(sketch_term(blocks, right), 'col')]
    pallas_call x0 -> x1, Pallas kernels: none -> 292 us  [local(): pl.pallas_call(kernel, out_shape=(jax.ShapeDtypeStruct((2, ROWS, RANK), j...]
    another operation x26 -> x0, other arithmetic: 245 us -> none  [the longest x17 146 us: orthonormal(): lower = jnp.linalg.cholesky(gram_total)]
    all_to_all x1 -> x0, blocking collectives: 105 us -> none  [local(): lax.all_to_all(base_flat, 'col', split_axis=2, concat_axis=1, tiled=True)]
    all_to_all x1 -> x0, waiting for transfers between devices: 104 us -> none  [local(): lax.all_to_all(adjusted_flat, 'col', split_axis=2, concat_axis=1, tiled=T...]
    unnamed x7 -> x0, waiting for transfers between devices: 71.2 us -> none
    dot_general x10 -> x0, matrix products: 53.3 us -> none  [the longest x2 36.6 us: gram_of(): jnp.einsum('rmk,rml->mkl', panel_three, panel_three, precision=lax.Precis...]
    unnamed x36 -> x4, local copies, waits for them, and re-layouts: 62 us -> 19.9 us
  transfers between devices with their start and end apart: 7 -> 0, of which waited for: 7 -> 0; matrix products, arithmetic and copies ran while one was open for 2% -> 0% of each run, Pallas kernels for 0% -> 0%
where the time goes in v1:
time: 317 us
  Pallas kernels  292 us (92%)
  local copies, waits for them, and re-layouts  23.9 us (8%)
    pallas_call x1, Pallas kernels, local(): pl.pallas_call(kernel, out_shape=(jax.ShapeDtypeStruct((2, ROWS, RANK), j...  292 us
    unnamed x4, local copies, waits for them, and re-layouts  19.9 us

profile of v1, /device:TPU:0, one launch (start us, length us, event | category | flops | bytes accessed | tf_op | source)
XLA Modules:
  0.0 316.8 jit_solution(4324039550028565953)
XLA Ops:
  0.6 0.0 copy-start
  0.6 11.6 %copy.5.base = bf16[2,231,8192]{2,1,0:T(8,128)(2,1)} copy(bf16[2,231,8192]{2,0,1:T(2,128)(2,1)} %param.3) | data formatting | bytes 15138816 | tf_op args[0]
  12.3 0.0 copy-done
  12.3 8.3 %copy.6.adjusted = bf16[2,231,8192]{2,1,0:T(8,128)(2,1)} copy(bf16[2,231,8192]{2,0,1:T(2,128)(2,1)S(1)} %copy-done) | data formatting | bytes 15138816 | tf_op args[1]
  20.6 292.3 %shard_map.50 = (f32[2,231,256]{2,1,0:T(8,128)}, f32[2,512,32]{2,1,0:T(8,128)}) custom-call(bf16[2,231,8192]{2,1,0:T(8,128)(2,1)} %copy.5.base, bf16[2,231,8192]{2,1,0:T(8,128)(2,1)} %copy.6.adjusted, bf16[2,512,256]{2,1,0:T(8,128)(2,1)} %omega.1), custom_call_target="tpu_custom_call" | custom-call | tf_op jit(solution)/shard_map/pallas_call | solution.py:412
  312.9 2.0 copy.7
  314.9 1.9 copy.8
Async XLA Ops:
  0.6 11.6 %copy-start = (bf16[2,231,8192]{2,0,1:T(2,128)(2,1)S(1)}, bf16[2,231,8192]{2,0,1:T(2,128)(2,1)}, u32[]{:S(2)}) copy-start(bf16[2,231,8192]{2,0,1:T(2,128)(2,1)} %param.4) | copy-start | bytes 22708228

commit v2 on v1

--- a/solution.py
+++ b/solution.py
@@ -14,6 +14,7 @@
 ORDERS = ((0, 1, 2), (1, 2, 0), (2, 0, 1))
 CUT_RS = ((0, 96), (96, 80), (176, 80))
 CUT_AG = ((0, 48), (48, 48), (96, 32))
+ORDERS_MAP = ((1, 0, 2), (1, 2, 0), (0, 2, 1))
 
 
 def dot(a, b, ca, cb, precision=None):
@@ -23,21 +24,28 @@
     size = 128
     lane = lax.broadcasted_iota(jnp.int32, (NB, size), 1)
     sub = lax.broadcasted_iota(jnp.int32, (NB, size), 0)
+
+    def wide(row):
+        return jnp.broadcast_to(row, (NB, size))
+
     def step(k, carry):
         start = pl.multiple_of(k * NB, NB)
-        rows = work[pl.ds(start, NB), :]
-        x = pltpu.roll(rows[:, :size], lax.rem(size - start, size), 1)
-        x = jnp.where(lane < NB, x, jnp.where(lane == sub + NB, 1.0, 0.0))
+        left, right = work[pl.ds(start, NB), :size], work[pl.ds(start, NB), size:]
+        block = pltpu.roll(left, lax.rem(size - start, size), 1)
+        cols = [wide(block[:, j : j + 1]) for j in range(NB)]
+        diag = cols[0]
         for j in range(NB - 1):
-            inv = 1.0 / x[j : j + 1, j : j + 1]
-            mult = x[:, j : j + 1] * inv
-            mult = jnp.where(sub > j, jnp.broadcast_to(mult, (NB, size)), 0.0)
-            x = x - mult * jnp.broadcast_to(x[j : j + 1, :], (NB, size))
-        diag = jnp.sum(jnp.where(lane == sub, x, 0.0), axis=1, keepdims=True)
-        t = x[:, NB : 2 * NB] * lax.rsqrt(diag)
-        new = dot(t, rows, 1, 0, HI)
-        left = jnp.where(lane >= start + NB, new[:, :size], 0.0)
-        work[...] -= dot(left, new, 0, 0, HI)
+            mult = jnp.where(sub > j, cols[j] * wide(1.0 / cols[j][j : j + 1, :]), 0.0)
+            for n in range(j + 1, NB):
+                cols[n] = cols[n] - mult * wide(cols[n][j : j + 1, :])
+            left = left - mult * wide(left[j : j + 1, :])
+            right = right - mult * wide(right[j : j + 1, :])
+            diag = jnp.where(sub > j, cols[j + 1], diag)
+        scale = lax.rsqrt(diag)
+        left, right = left * scale, right * scale
+        below = jnp.where(lane >= start + NB, left, 0.0)
+        new = jnp.concatenate([left, right], axis=1)
+        work[...] -= dot(below, new, 0, 0, HI)
         work[pl.ds(start, NB), :] = new
         return carry
     lax.fori_loop(0, size // NB, step, 0)
@@ -76,7 +84,7 @@
     )
 
 
-def reduce_scatter(pos, core, source, bufs, total, send_sems, recv_sems):
+def reduce_scatter(pos, core, source, fill, bufs, total, send_sems, recv_sems, slab_sems):
     copies = {}
 
     def launch(part, stage, block):
@@ -113,7 +121,35 @@
             copy.wait_recv()
 
     for part in range(3):
-        launch(part, 0, lambda at, part=part: first(part, at))
+        copies[part, 0] = []
+    for slab in (2, 1, 3, 0):
+        x = lax.rem(pos[0] + slab, 4)
+        fill(x)
+        if slab:
+            copy = send(
+                first(0, x),
+                bufs[0][0].at[slab - 1],
+                send_sems.at[0, 0, slab - 1],
+                recv_sems.at[0, 0, slab - 1],
+                device_at(moved(pos, 0, slab), core),
+            )
+            copy.start()
+            copies[0, 0].append(copy)
+        for part in (1, 2):
+            start, size = CUT_RS[part]
+            rows = pl.ds(start, size)
+            for step in (2, 1, 3):
+                to = moved(pos, part, step)
+                block = source.at[x, to[1], :, rows] if part == 1 else source.at[x, :, to[2], rows]
+                copy = send(
+                    block,
+                    bufs[part][0].at[step - 1, x],
+                    slab_sems.at[0, part - 1, slab, step - 1],
+                    slab_sems.at[1, part - 1, x, step - 1],
+                    device_at(to, core),
+                )
+                copy.start()
+                copies[part, 0].append(copy)
     for part in range(3):
         arrived(part, 0)
         here, got, held = first(part, pos[ORDERS[part][0]]), bufs[part][0], bufs[part][1]
@@ -218,75 +254,115 @@
 
 def kernel(base, adjusted, omega, up, down, *scratch):
     (
-        load_base, load_adjusted, load_sems, delta, outgoing, delta_sems, sketch_map, map_sems,
+        load_base, load_adjusted, load_sems, apart, delta, outgoing, delta_sems, sketch_map, map_sems,
         sketch, sketch_got, power, power_got, swap_sems, turned, source,
         *rest,
     ) = scratch
     bufs = [rest[5 * part : 5 * part + 5] for part in range(3)]
     (
-        total, rs_send, rs_recv, columns, ag_send, ag_recv,
+        total, rs_send, rs_recv, slab_sems, columns, ag_send, ag_recv,
         pieces, gram_got, gram_mine, gram, gram_sems, work, factor, spread, spread_send, spread_recv,
     ) = rest[15:]
     row, col = lax.axis_index("row"), lax.axis_index("col")
     core = lax.rem(col, 2)
     pos = (lax.div(col, 4), lax.rem(lax.div(col, 2), 2) * 2 + lax.div(row, 4), lax.rem(row, 4))
     mate = device_at(pos, 1 - core)
-    own = lax.div(col, 2)
-    chip = pos[0] * 16 + pos[1] * 4 + pos[2]
+
+    yh = lax.div(pos[1], 2)
+    spot = (pos[0], yh, pos[2])
 
     def load(n):
-        slot = n % 4
-        block = 2 * (n % 8) + ((1 - core) if n < 8 else core)
-        lanes = pl.ds(pl.multiple_of(block * WIDE, WIDE), WIDE)
-        return (
-            pltpu.make_async_copy(base.at[:, :, lanes], load_base.at[slot], load_sems.at[slot, 0]),
-            pltpu.make_async_copy(adjusted.at[:, :, lanes], load_adjusted.at[slot], load_sems.at[slot, 1]),
-        )
+        slot = lax.rem(n, 4)
+        block = 2 * lax.rem(n, 8) + jnp.where(n < 8, 1 - core, core)
+        copies = []
+        for tile in range(4):
+            lanes = pl.ds(pl.multiple_of(block * WIDE + tile * SUB, SUB), SUB)
+            for which, (array, held) in enumerate(((base, load_base), (adjusted, load_adjusted))):
+                copies.append(
+                    pltpu.make_async_copy(array.at[:, :, lanes], held.at[slot, tile], load_sems.at[slot, which, tile])
+                )
+        return copies
 
     for n in range(4):
         for copy in load(n):
             copy.start()
-    own_map = pltpu.make_async_copy(omega, sketch_map.at[own], map_sems.at[14])
+    quarter = pl.ds(pl.multiple_of(pos[2] * SUB, SUB), SUB)
+    own_map = pltpu.make_async_copy(omega.at[:, quarter], sketch_map.at[spot], map_sems.at[0, 0, 0, 0])
     own_map.start()
 
     barrier = pltpu.get_barrier_semaphore()
-    pl.semaphore_signal(barrier, 1, device_id=mate, device_id_type=MESH)
-
-    @pl.loop(1, 64)
-    def _(step):
-        to = lax.rem(chip + step, 64)
-        device = device_at((lax.div(to, 16), lax.rem(lax.div(to, 4), 4), lax.rem(to, 4)), core)
+    near = [moved(pos, axis, step) for axis in (0, 2) for step in (1, 2, 3)]
+    near += [(pos[0], 3 - pos[1], pos[2]), (pos[0], pos[1] + 1 - 2 * lax.rem(pos[1], 2), pos[2])]
+    for device in [mate] + [device_at(to, core) for to in near]:
         pl.semaphore_signal(barrier, 1, device_id=device, device_id_type=MESH)
-
-    pl.semaphore_wait(barrier, 64)
-
-    map_copies = []
-    for step in range(1, 8):
-        far = (lax.rem(pos[0] + step // 2, 4), lax.rem(pos[1] + 2 * (step % 2), 4), pos[2])
-        copy = send(omega, sketch_map.at[own], map_sems.at[step - 1], map_sems.at[step + 6], device_at(far, core))
-        copy.start()
-        map_copies.append(copy)
-
-    delta_copies = []
+    pl.semaphore_wait(barrier, 9)
+
+    map_copies = {}
+
+    def launch_map(stage):
+        for part in range(3):
+            start, size = CUT_AG[part]
+            order = ORDERS_MAP[part]
+            if stage:
+                for copy in map_copies[part, stage - 1]:
+                    copy.wait_recv()
+            index = tuple(slice(None) if a in order[:stage] else spot[a] for a in range(3))
+            block = sketch_map.at[index + (slice(None), pl.ds(start, size))]
+            axis = order[stage]
+            map_copies[part, stage] = []
+            for step in (2, 1, 3) if axis != 1 else (1,):
+                to = (pos[0], 3 - pos[1], pos[2]) if axis == 1 else moved(pos, axis, step)
+                copy = send(
+                    block,
+                    block,
+                    map_sems.at[1, part, stage, step - 1],
+                    map_sems.at[2, part, stage, step - 1],
+                    device_at(to, core),
+                )
+                copy.start()
+                map_copies[part, stage].append(copy)
+
+    own_map.wait()
+    launch_map(0)
     zeros = jnp.zeros((2, PAD - 224, WIDE), jnp.bfloat16)
-    for n in range(16):
-        for copy in load(n):
-            copy.wait()
-        place = outgoing.at[n] if n < 8 else delta.at[n - 8, core]
-        place[:, 224:, :] = zeros
-        for m in range(2):
-            value = load_adjusted[n % 4, m].astype(jnp.float32) - load_base[n % 4, m].astype(jnp.float32)
-            place[m, 0:ROWS, :] = value.astype(jnp.bfloat16)
-        if n < 12:
-            for copy in load(n + 4):
-                copy.start()
-        if n < 8:
-            copy = send(outgoing.at[n], delta.at[n, core], delta_sems.at[0, n], delta_sems.at[1, n], mate)
-            copy.start()
-            delta_copies.append(copy)
-    own_map.wait()
-    for copy in map_copies + delta_copies:
-        copy.wait()
+
+    def subtract(low, high, leaving):
+        @pl.loop(low, high)
+        def _(n):
+            slot = lax.rem(n, 4)
+            for copy in load(n):
+                copy.wait()
+            place = outgoing.at[n] if leaving else delta.at[n - 8, core]
+            place[:, 224:, :] = zeros
+            for tile in range(4):
+                value = load_adjusted[slot, tile].astype(jnp.float32) - load_base[slot, tile].astype(jnp.float32)
+                apart[tile, 0 : 2 * ROWS] = value.reshape(2 * ROWS, SUB)
+                for m in range(2):
+                    rows = apart[tile, pl.ds(m, ROWS, stride=2), :]
+                    place[m, 0:ROWS, tile * SUB : (tile + 1) * SUB] = rows.astype(jnp.bfloat16)
+
+            @pl.when(n < 12)
+            def _():
+                for copy in load(n + 4):
+                    copy.start()
+
+            if leaving:
+                send(outgoing.at[n], delta.at[n, core], delta_sems.at[0, n], delta_sems.at[1, n], mate).start()
+
+    subtract(0, 3, True)
+    launch_map(1)
+    subtract(3, 8, True)
+    subtract(8, 9, False)
+    launch_map(2)
+    subtract(9, 16, False)
+    for n in range(8):
+        send(outgoing.at[n], delta.at[n, core], delta_sems.at[0, n], delta_sems.at[1, n], mate).wait()
+    for part in range(3):
+        for copy in map_copies[part, 2]:
+            copy.wait_recv()
+    for copies in map_copies.values():
+        for copy in copies:
+            copy.wait_send()
 
     def swap(part, got, which):
         copy = send(part, got, swap_sems.at[0, which], swap_sems.at[1, which], mate)
@@ -302,15 +378,15 @@
                 part[m] += dot(delta[i, :, m].reshape(2 * PAD, WIDE), right(i, m), 1, 0)
 
     def folded():
-        for m in range(2):
-
-            @pl.loop(0, 8)
-            def _(i, m=m):
-                value = dot(turned[m], delta[i, :, m].reshape(2 * PAD, WIDE), 1, 0).astype(jnp.bfloat16)
-                for z in range(4):
-                    source[lax.div(i, 2), lax.rem(i, 2) * 2 + m, z] = value[:, z * SUB : (z + 1) * SUB]
-
-        reduce_scatter(pos, core, source, bufs, total, rs_send, rs_recv)
+        def fill(x):
+            @pl.loop(0, 2)
+            def _(n):
+                for m in range(2):
+                    value = dot(turned[m], delta[x * 2 + n, :, m].reshape(2 * PAD, WIDE), 1, 0).astype(jnp.bfloat16)
+                    for z in range(4):
+                        source[x, n * 2 + m, z] = value[:, z * SUB : (z + 1) * SUB]
+
+        reduce_scatter(pos, core, source, fill, bufs, total, rs_send, rs_recv, slab_sems)
 
     def orthonormal(panel, which):
         gram_sum(pos, core, panel[core], pieces, gram_got, gram_mine, gram, gram_sems)
@@ -319,7 +395,7 @@
         for m in range(2):
             turned[m] = dot(factor[m], panel[m], 1, 1, HI).astype(jnp.bfloat16)
 
-    product(lambda i, m: sketch_map[i, m], sketch)
+    product(lambda i, m: sketch_map[lax.div(i, 2), lax.rem(i, 2), :, m].reshape(WIDE, RANK), sketch)
     swap(sketch, sketch_got, 0)
     sketch[...] += sketch_got[...]
     orthonormal(sketch, 1)
@@ -335,7 +411,7 @@
     orthonormal(power, 3)
     for m in range(2):
         rows = power[m, pl.ds(pl.multiple_of(core * PAD, PAD), PAD), :]
-        up[m] = (dot(rows, factor[m], 1, 1, HI) * math.sqrt(29568))[:ROWS]
+        up[:, m, :] = (dot(rows, factor[m], 1, 1, HI) * math.sqrt(29568))[:ROWS]
     folded()
 
     spread_copies = []
@@ -355,7 +431,7 @@
     for copy in spread_copies:
         copy.wait()
     for n in range(8):
-        down[n // 4, (n % 4) * SUB : (n % 4 + 1) * SUB, :] = spread[n].T
+        down[n // 4, :, (n % 4) * SUB : (n % 4 + 1) * SUB] = spread[n]
 
 
 def scratch_shapes():
@@ -371,14 +447,15 @@
             pltpu.VMEM((3, size, SUB), half),
         ]
     return [
-        pltpu.VMEM((4, 2, ROWS, WIDE), half),
-        pltpu.VMEM((4, 2, ROWS, WIDE), half),
-        dma((4, 2)),
+        pltpu.VMEM((4, 4, ROWS, 2, SUB), half),
+        pltpu.VMEM((4, 4, ROWS, 2, SUB), half),
+        dma((4, 2, 4)),
+        pltpu.VMEM((4, 2 * PAD, SUB), full),
         pltpu.VMEM((8, 2, 2, PAD, WIDE), half),
         pltpu.VMEM((8, 2, PAD, WIDE), half),
         dma((2, 8)),
-        pltpu.VMEM((8, 2, WIDE, RANK), half),
-        dma((15,)),
+        pltpu.VMEM((4, 2, 4, 2, SUB, RANK), half),
+        dma((3, 3, 3, 3)),
         pltpu.VMEM((2, 2 * PAD, RANK), full),
         pltpu.VMEM((2, 2 * PAD, RANK), full),
         pltpu.VMEM((2, 2 * PAD, RANK), full),
@@ -390,6 +467,7 @@
         pltpu.VMEM((RANK, SUB), full),
         dma((3, 3, 3)),
         dma((3, 3, 3)),
+        dma((2, 2, 4, 3)),
         pltpu.VMEM((4, 4, 4, SUB, RANK), half),
         dma((3, 3, 3)),
         dma((3, 3, 3)),
@@ -409,11 +487,11 @@
 def local(base_flat, adjusted_flat, omega):
     anywhere = pl.BlockSpec(memory_space=pl.ANY)
     vmem = pl.BlockSpec(memory_space=pltpu.VMEM)
-    return pl.pallas_call(
+    up, down = pl.pallas_call(
         kernel,
         out_shape=(
-            jax.ShapeDtypeStruct((2, ROWS, RANK), jnp.float32),
-            jax.ShapeDtypeStruct((2, WIDE, 32), jnp.float32),
+            jax.ShapeDtypeStruct((ROWS, 2, RANK), jnp.float32),
+            jax.ShapeDtypeStruct((2, 32, WIDE), jnp.float32),
         ),
         in_specs=[anywhere] * 3,
         out_specs=(vmem, vmem),
@@ -421,7 +499,8 @@
         compiler_params=pltpu.CompilerParams(
             collective_id=0, has_side_effects=True, vmem_limit_bytes=60 * 2**20
         ),
-    )(base_flat, adjusted_flat, omega)
+    )(base_flat.transpose(1, 0, 2), adjusted_flat.transpose(1, 0, 2), omega)
+    return up.transpose(1, 0, 2), down.transpose(0, 2, 1)
 
 
 def solution(mesh):

time: 317 us -> 218 us (0.69)
  Pallas kernels: 292 us -> 213 us
  local copies, waits for them, and re-layouts: 23.9 us -> 3.53 us
    pallas_call x1, Pallas kernels: 292 us -> 213 us  [local(): pl.pallas_call(kernel, out_shape=(jax.ShapeDtypeStruct((ROWS, 2, RANK), j...]
    unnamed x4 -> x2, local copies, waits for them, and re-layouts: 19.9 us -> 3.53 us
    pallas_call x2 -> x0, local copies, waits for them, and re-layouts: 3.91 us -> none  [local(): pl.pallas_call(kernel, out_shape=(jax.ShapeDtypeStruct((2, ROWS, RANK), j...]
where the time goes in v2:
time: 218 us; the launch traced here: 217 us
  Pallas kernels  213 us (98%)
  local copies, waits for them, and re-layouts  3.53 us (2%)
    pallas_call x1, Pallas kernels, local(): pl.pallas_call(kernel, out_shape=(jax.ShapeDtypeStruct((ROWS, 2, RANK), j...  213 us

profile of v2, /device:TPU:0, one launch (start us, length us, event | category | flops | bytes accessed | tf_op | source)
XLA Modules:
  0.0 217.5 jit_solution(3382368038342831910)
XLA Ops:
  0.6 213.3 %shard_map.50 = (f32[231,2,256]{2,1,0:T(2,128)}, f32[2,32,512]{2,1,0:T(8,128)}) custom-call(bf16[231,2,8192]{2,1,0:T(2,128)(2,1)} %bitcast.4, bf16[231,2,8192]{2,1,0:T(2,128)(2,1)} %bitcast.5, bf16[2,512,256]{2,1,0:T(8,128)(2,1)} %omega.1), custom_call_target="tpu_custom_call" | custom-call | tf_op jit(solution)/shard_map/pallas_call | solution.py:490
  213.9 2.0 copy.7
  215.9 1.6 copy.8

commit v3 on v2

--- a/solution.py
+++ b/solution.py
@@ -11,18 +11,24 @@
 MESH = pl.DeviceIdType.MESH
 NB = 16
 ROWS, PAD, WIDE, RANK, SUB = 231, 240, 512, 256, 128
-ORDERS = ((0, 1, 2), (1, 2, 0), (2, 0, 1))
-CUT_RS = ((0, 96), (96, 80), (176, 80))
-CUT_AG = ((0, 48), (48, 48), (96, 32))
-ORDERS_MAP = ((1, 0, 2), (1, 2, 0), (0, 2, 1))
+ORDERS = ((0, 1, 2), (1, 2, 0), (2, 0, 1)) * 2
+CUT_RS = ((0, 48), (48, 32), (80, 48), (128, 48), (176, 48), (224, 32))
+CUT_AG = ((0, 16), (16, 16), (32, 16), (48, 32), (80, 32), (112, 16))
+PARTS = range(6)
 
 
 def dot(a, b, ca, cb, precision=None):
     return lax.dot_general(a, b, (((ca,), (cb,)), ((), ())), precision=precision, preferred_element_type=jnp.float32)
 
+def terms(value):
+    high = value.astype(jnp.bfloat16)
+    rest = value - high.astype(jnp.float32)
+    middle = rest.astype(jnp.bfloat16)
+    return high, middle, (rest - middle.astype(jnp.float32)).astype(jnp.bfloat16)
+
+
 def factor_panel(work):
     size = 128
-    lane = lax.broadcasted_iota(jnp.int32, (NB, size), 1)
     sub = lax.broadcasted_iota(jnp.int32, (NB, size), 0)
 
     def wide(row):
@@ -43,9 +49,12 @@
             diag = jnp.where(sub > j, cols[j + 1], diag)
         scale = lax.rsqrt(diag)
         left, right = left * scale, right * scale
-        below = jnp.where(lane >= start + NB, left, 0.0)
         new = jnp.concatenate([left, right], axis=1)
-        work[...] -= dot(below, new, 0, 0, HI)
+        high, middle, low = terms(new)
+        ahead = jnp.where(lax.broadcasted_iota(jnp.int32, (6 * NB, size), 1) >= start + NB, 1.0, 0.0).astype(jnp.bfloat16)
+        below = jnp.concatenate([t[:, :size] for t in (high, high, middle, high, low, middle)], axis=0) * ahead
+        other = jnp.concatenate([high, middle, high, low, high, middle], axis=0)
+        work[...] -= dot(below, other, 0, 0)
         work[pl.ds(start, NB), :] = new
         return carry
     lax.fori_loop(0, size // NB, step, 0)
@@ -84,86 +93,74 @@
     )
 
 
-def reduce_scatter(pos, core, source, fill, bufs, total, send_sems, recv_sems, slab_sems):
-    copies = {}
+def reduce_scatter(pos, core, source, fill, bufs, total, send_sems, recv_sems, slab_sems, between):
+    copies = {(part, 0): [] for part in PARTS}
+
+    def begin(part, stage, src, dst, sem, step):
+        copy = send(src, dst, *sem, device_at(moved(pos, ORDERS[part][stage], step), core))
+        copy.start()
+        copies[part, stage].append(copy)
 
     def launch(part, stage, block):
         axis = ORDERS[part][stage]
         copies[part, stage] = []
         for step in (2, 1, 3):
-            to = moved(pos, axis, step)
-            copy = send(
-                block(to[axis]),
-                bufs[part][2 * stage].at[step - 1],
-                send_sems.at[part, stage, step - 1],
-                recv_sems.at[part, stage, step - 1],
-                device_at(to, core),
-            )
-            copy.start()
-            copies[part, stage].append(copy)
-
-    def first(part, at):
-        start, size = CUT_RS[part]
-        rows = pl.ds(start, size)
+            sem = (send_sems.at[part, stage, step - 1], recv_sems.at[part, stage, step - 1])
+            begin(part, stage, block(moved(pos, axis, step)[axis]), bufs[part][2 * stage].at[step - 1], sem, step)
+
+    def slab_out(part, slab, x):
+        rows = pl.ds(*CUT_RS[part])
         axis = ORDERS[part][0]
         if axis == 0:
-            return source.at[at, :, :, rows]
-        if axis == 1:
-            return source.at[:, at, :, rows]
-        return source.at[:, :, at, rows]
+            if slab:
+                sem = (send_sems.at[part, 0, slab - 1], recv_sems.at[part, 0, slab - 1])
+                begin(part, 0, source.at[x, :, :, rows], bufs[part][0].at[slab - 1], sem, slab)
+            return
+        for step in (2, 1, 3):
+            to = moved(pos, axis, step)
+            block = source.at[x, to[1], :, rows] if axis == 1 else source.at[x, :, to[2], rows]
+            sem = (slab_sems.at[0, part, slab, step - 1], slab_sems.at[1, part, x, step - 1])
+            begin(part, 0, block, bufs[part][0].at[step - 1, x], sem, step)
+
+    def own(part):
+        rows = pl.ds(*CUT_RS[part])
+        return (
+            lambda a, b: source.at[pos[0], a, b, rows],
+            lambda a, b: source.at[a, pos[1], b, rows],
+            lambda a, b: source.at[a, b, pos[2], rows],
+        )[ORDERS[part][0]]
 
     def second(part, at):
         held = bufs[part][1]
-        return held.at[:, at] if part == 1 else held.at[at]
+        return held.at[:, at] if ORDERS[part][0] == 1 else held.at[at]
 
     def arrived(part, stage):
         for copy in copies[part, stage]:
             copy.wait_recv()
 
-    for part in range(3):
-        copies[part, 0] = []
-    for slab in (2, 1, 3, 0):
-        x = lax.rem(pos[0] + slab, 4)
+    slabs = [(slab, lax.rem(pos[0] + slab, 4)) for slab in (2, 1, 3, 0)]
+    for slab, x in slabs:
         fill(x)
-        if slab:
-            copy = send(
-                first(0, x),
-                bufs[0][0].at[slab - 1],
-                send_sems.at[0, 0, slab - 1],
-                recv_sems.at[0, 0, slab - 1],
-                device_at(moved(pos, 0, slab), core),
-            )
-            copy.start()
-            copies[0, 0].append(copy)
-        for part in (1, 2):
-            start, size = CUT_RS[part]
-            rows = pl.ds(start, size)
-            for step in (2, 1, 3):
-                to = moved(pos, part, step)
-                block = source.at[x, to[1], :, rows] if part == 1 else source.at[x, :, to[2], rows]
-                copy = send(
-                    block,
-                    bufs[part][0].at[step - 1, x],
-                    slab_sems.at[0, part - 1, slab, step - 1],
-                    slab_sems.at[1, part - 1, x, step - 1],
-                    device_at(to, core),
-                )
-                copy.start()
-                copies[part, 0].append(copy)
-    for part in range(3):
+        for part in range(3):
+            slab_out(part, slab, x)
+    for slab, x in slabs:
+        for part in range(3, 6):
+            slab_out(part, slab, x)
+    between()
+    for part in PARTS:
         arrived(part, 0)
-        here, got, held = first(part, pos[ORDERS[part][0]]), bufs[part][0], bufs[part][1]
+        here, got, held = own(part), bufs[part][0], bufs[part][1]
 
         @pl.loop(0, 16)
         def _(n, here=here, got=got, held=held):
             a, b = lax.div(n, 4), lax.rem(n, 4)
-            value = here[a, b].astype(jnp.float32)
+            value = here(a, b)[...].astype(jnp.float32)
             for step in range(3):
                 value += got[step, a, b].astype(jnp.float32)
             held[a, b] = value.astype(jnp.bfloat16)
 
         launch(part, 1, lambda at, part=part: second(part, at))
-    for part in range(3):
+    for part in PARTS:
         arrived(part, 1)
         here, got, held = second(part, pos[ORDERS[part][1]]), bufs[part][2], bufs[part][3]
         for a in range(4):
@@ -172,52 +169,49 @@
                 value += got[step, a].astype(jnp.float32)
             held[a] = value.astype(jnp.bfloat16)
         launch(part, 2, lambda at, held=held: held.at[at])
-    for part in range(3):
+    for part in PARTS:
         arrived(part, 2)
-        start, size = CUT_RS[part]
         value = bufs[part][3][pos[ORDERS[part][2]]].astype(jnp.float32)
         for step in range(3):
             value += bufs[part][4][step].astype(jnp.float32)
-        total[start : start + size, :] = value
-    for part in range(3):
-        for stage in range(3):
-            for copy in copies[part, stage]:
-                copy.wait_send()
+        total[pl.ds(*CUT_RS[part]), :] = value
+    for started in copies.values():
+        for copy in started:
+            copy.wait_send()
 
 
 def all_gather(pos, core, blocks, send_sems, recv_sems):
     copies = {}
 
-    def launch(part, stage):
-        start, size = CUT_AG[part]
-        done = ORDERS[part][:stage]
-        index = tuple(slice(None) if a in done else pos[a] for a in range(3)) + (pl.ds(start, size),)
-        axis = ORDERS[part][stage]
-        copies[part, stage] = []
-        for step in (2, 1, 3):
-            copy = send(
-                blocks.at[index],
-                blocks.at[index],
-                send_sems.at[part, stage, step - 1],
-                recv_sems.at[part, stage, step - 1],
-                device_at(moved(pos, axis, step), core),
-            )
-            copy.start()
-            copies[part, stage].append(copy)
-
-    for stage in range(3):
-        for part in range(3):
+    def launch(stage):
+        for part in PARTS:
             if stage:
                 for copy in copies[part, stage - 1]:
                     copy.wait_recv()
-            launch(part, stage)
-    for part in range(3):
-        for copy in copies[part, 2]:
-            copy.wait_recv()
-    for part in range(3):
-        for stage in range(3):
-            for copy in copies[part, stage]:
+            done = ORDERS[part][:stage]
+            index = tuple(slice(None) if a in done else pos[a] for a in range(3)) + (pl.ds(*CUT_AG[part]),)
+            axis = ORDERS[part][stage]
+            copies[part, stage] = []
+            for step in (2, 1, 3):
+                copy = send(
+                    blocks.at[index],
+                    blocks.at[index],
+                    send_sems.at[part, stage, step - 1],
+                    recv_sems.at[part, stage, step - 1],
+                    device_at(moved(pos, axis, step), core),
+                )
+                copy.start()
+                copies[part, stage].append(copy)
+
+    def finish():
+        for part in PARTS:
+            for copy in copies[part, 2]:
+                copy.wait_recv()
+        for started in copies.values():
+            for copy in started:
                 copy.wait_send()
+
+    return launch, finish
 
 
 def gram_sum(pos, core, panel, pieces, got, mine, whole, sems):
@@ -255,21 +249,18 @@
 def kernel(base, adjusted, omega, up, down, *scratch):
     (
         load_base, load_adjusted, load_sems, apart, delta, outgoing, delta_sems, sketch_map, map_sems,
-        sketch, sketch_got, power, power_got, swap_sems, turned, source,
+        sketch, sketch_got, power, power_got, panel, swap_sems, turned, source,
         *rest,
     ) = scratch
-    bufs = [rest[5 * part : 5 * part + 5] for part in range(3)]
+    bufs = [rest[5 * part : 5 * part + 5] for part in PARTS]
     (
         total, rs_send, rs_recv, slab_sems, columns, ag_send, ag_recv,
         pieces, gram_got, gram_mine, gram, gram_sems, work, factor, spread, spread_send, spread_recv,
-    ) = rest[15:]
+    ) = rest[30:]
     row, col = lax.axis_index("row"), lax.axis_index("col")
     core = lax.rem(col, 2)
     pos = (lax.div(col, 4), lax.rem(lax.div(col, 2), 2) * 2 + lax.div(row, 4), lax.rem(row, 4))
     mate = device_at(pos, 1 - core)
-
-    yh = lax.div(pos[1], 2)
-    spot = (pos[0], yh, pos[2])
 
     def load(n):
         slot = lax.rem(n, 4)
@@ -286,43 +277,25 @@
     for n in range(4):
         for copy in load(n):
             copy.start()
-    quarter = pl.ds(pl.multiple_of(pos[2] * SUB, SUB), SUB)
-    own_map = pltpu.make_async_copy(omega.at[:, quarter], sketch_map.at[spot], map_sems.at[0, 0, 0, 0])
-    own_map.start()
+    eighth = pl.ds(pl.multiple_of(pos[2] * SUB + lax.rem(pos[1], 2) * 64, 64), 64)
+    own_map = [
+        pltpu.make_async_copy(
+            omega.at[m, eighth], sketch_map.at[pos[0], pos[1], pos[2], pl.ds(m * 64, 64)], map_sems.at[m]
+        )
+        for m in range(2)
+    ]
+    for copy in own_map:
+        copy.start()
 
     barrier = pltpu.get_barrier_semaphore()
-    near = [moved(pos, axis, step) for axis in (0, 2) for step in (1, 2, 3)]
-    near += [(pos[0], 3 - pos[1], pos[2]), (pos[0], pos[1] + 1 - 2 * lax.rem(pos[1], 2), pos[2])]
+    near = [moved(pos, axis, step) for axis in range(3) for step in (1, 2, 3)]
     for device in [mate] + [device_at(to, core) for to in near]:
         pl.semaphore_signal(barrier, 1, device_id=device, device_id_type=MESH)
-    pl.semaphore_wait(barrier, 9)
-
-    map_copies = {}
-
-    def launch_map(stage):
-        for part in range(3):
-            start, size = CUT_AG[part]
-            order = ORDERS_MAP[part]
-            if stage:
-                for copy in map_copies[part, stage - 1]:
-                    copy.wait_recv()
-            index = tuple(slice(None) if a in order[:stage] else spot[a] for a in range(3))
-            block = sketch_map.at[index + (slice(None), pl.ds(start, size))]
-            axis = order[stage]
-            map_copies[part, stage] = []
-            for step in (2, 1, 3) if axis != 1 else (1,):
-                to = (pos[0], 3 - pos[1], pos[2]) if axis == 1 else moved(pos, axis, step)
-                copy = send(
-                    block,
-                    block,
-                    map_sems.at[1, part, stage, step - 1],
-                    map_sems.at[2, part, stage, step - 1],
-                    device_at(to, core),
-                )
-                copy.start()
-                map_copies[part, stage].append(copy)
-
-    own_map.wait()
+    pl.semaphore_wait(barrier, 10)
+
+    launch_map, finish_map = all_gather(pos, core, sketch_map, ag_send, ag_recv)
+    for copy in own_map:
+        copy.wait()
     launch_map(0)
     zeros = jnp.zeros((2, PAD - 224, WIDE), jnp.bfloat16)
 
@@ -357,27 +330,37 @@
     subtract(9, 16, False)
     for n in range(8):
         send(outgoing.at[n], delta.at[n, core], delta_sems.at[0, n], delta_sems.at[1, n], mate).wait()
-    for part in range(3):
-        for copy in map_copies[part, 2]:
-            copy.wait_recv()
-    for copies in map_copies.values():
-        for copy in copies:
-            copy.wait_send()
+    finish_map()
 
     def swap(part, got, which):
         copy = send(part, got, swap_sems.at[0, which], swap_sems.at[1, which], mate)
         copy.start()
         copy.wait()
 
-    def product(right, part):
-        for m in range(2):
+    def product(right, part, got, which):
+        copies = []
+        for order, m in enumerate((1 - core, core)):
             part[m] = jnp.zeros((2 * PAD, RANK), jnp.float32)
 
             @pl.loop(0, 8)
             def _(i, m=m):
                 part[m] += dot(delta[i, :, m].reshape(2 * PAD, WIDE), right(i, m), 1, 0)
 
-    def folded():
+            copy = send(part.at[m], got.at[m], swap_sems.at[0, which + order], swap_sems.at[1, which + order], mate)
+            copy.start()
+            copies.append(copy)
+        copies[0].wait_recv()
+        panel[core] = part[core] + got[core]
+
+        def finish():
+            copies[1].wait_recv()
+            panel[1 - core] = part[1 - core] + got[1 - core]
+            for copy in copies:
+                copy.wait_send()
+
+        return finish
+
+    def folded(between):
         def fill(x):
             @pl.loop(0, 2)
             def _(n):
@@ -386,33 +369,41 @@
                     for z in range(4):
                         source[x, n * 2 + m, z] = value[:, z * SUB : (z + 1) * SUB]
 
-        reduce_scatter(pos, core, source, fill, bufs, total, rs_send, rs_recv, slab_sems)
-
-    def orthonormal(panel, which):
+        reduce_scatter(pos, core, source, fill, bufs, total, rs_send, rs_recv, slab_sems, between)
+
+    def orthonormal(finish, which):
         gram_sum(pos, core, panel[core], pieces, gram_got, gram_mine, gram, gram_sems)
+        finish()
         invert_factor(gram, work, factor.at[core])
         swap(factor.at[core], factor.at[core], which)
         for m in range(2):
             turned[m] = dot(factor[m], panel[m], 1, 1, HI).astype(jnp.bfloat16)
 
-    product(lambda i, m: sketch_map[lax.div(i, 2), lax.rem(i, 2), :, m].reshape(WIDE, RANK), sketch)
-    swap(sketch, sketch_got, 0)
-    sketch[...] += sketch_got[...]
-    orthonormal(sketch, 1)
-    folded()
+    def sketch_rows(i, m):
+        x, yh = lax.div(i, 2), lax.rem(i, 2)
+        rows = pl.ds(pl.multiple_of(m * 64, 64), 64)
+        return jnp.concatenate(
+            [sketch_map[x, yh * 2 + low, z, rows, :] for z in range(4) for low in range(2)], axis=0
+        )
+
+    def column_rows(i, m):
+        return columns[lax.div(i, 2), lax.rem(i, 2) * 2 + m].reshape(WIDE, RANK)
+
+    orthonormal(product(sketch_rows, sketch, sketch_got, 0), 4)
+    folded(lambda: None)
     columns[pos[0], pos[1], pos[2]] = total[...].T.astype(jnp.bfloat16)
-    all_gather(pos, core, columns, ag_send, ag_recv)
-    product(
-        lambda i, m: columns[lax.div(i, 2), lax.rem(i, 2) * 2 + m].reshape(WIDE, RANK),
-        power,
-    )
-    swap(power, power_got, 2)
-    power[...] += power_got[...]
-    orthonormal(power, 3)
-    for m in range(2):
-        rows = power[m, pl.ds(pl.multiple_of(core * PAD, PAD), PAD), :]
-        up[:, m, :] = (dot(rows, factor[m], 1, 1, HI) * math.sqrt(29568))[:ROWS]
-    folded()
+    launch, finish_columns = all_gather(pos, core, columns, ag_send, ag_recv)
+    for stage in range(3):
+        launch(stage)
+    finish_columns()
+    orthonormal(product(column_rows, power, power_got, 2), 5)
+
+    def adapter_up():
+        for m in range(2):
+            rows = panel[m, pl.ds(pl.multiple_of(core * PAD, PAD), PAD), :]
+            up[:, m, :] = (dot(rows, factor[m], 1, 1, HI) * math.sqrt(29568))[:ROWS]
+
+    folded(adapter_up)
 
     spread_copies = []
     for step in range(1, 8):
@@ -454,23 +445,24 @@
         pltpu.VMEM((8, 2, 2, PAD, WIDE), half),
         pltpu.VMEM((8, 2, PAD, WIDE), half),
         dma((2, 8)),
-        pltpu.VMEM((4, 2, 4, 2, SUB, RANK), half),
-        dma((3, 3, 3, 3)),
+        pltpu.VMEM((4, 4, 4, SUB, RANK), half),
+        dma((2,)),
         pltpu.VMEM((2, 2 * PAD, RANK), full),
         pltpu.VMEM((2, 2 * PAD, RANK), full),
         pltpu.VMEM((2, 2 * PAD, RANK), full),
         pltpu.VMEM((2, 2 * PAD, RANK), full),
-        dma((2, 4)),
+        pltpu.VMEM((2, 2 * PAD, RANK), full),
+        dma((2, 6)),
         pltpu.VMEM((2, RANK, 2 * PAD), half),
         pltpu.VMEM((4, 4, 4, RANK, SUB), half),
         *parts,
         pltpu.VMEM((RANK, SUB), full),
-        dma((3, 3, 3)),
-        dma((3, 3, 3)),
-        dma((2, 2, 4, 3)),
+        dma((6, 3, 3)),
+        dma((6, 3, 3)),
+        dma((2, 6, 4, 3)),
         pltpu.VMEM((4, 4, 4, SUB, RANK), half),
-        dma((3, 3, 3)),
-        dma((3, 3, 3)),
+        dma((6, 3, 3)),
+        dma((6, 3, 3)),
         pltpu.VMEM((64, 8, SUB), full),
         pltpu.VMEM((64, 8, SUB), full),
         pltpu.VMEM((8, SUB), full),

time: 218 us -> 200 us (0.917)
  Pallas kernels: 213 us -> 196 us
    pallas_call x1, Pallas kernels: 213 us -> 196 us  [local(): pl.pallas_call(kernel, out_shape=(jax.ShapeDtypeStruct((ROWS, 2, RANK), j...]
where the time goes in v3:
time: 200 us
  Pallas kernels  196 us (98%)
  local copies, waits for them, and re-layouts  3.53 us (2%)
    pallas_call x1, Pallas kernels, local(): pl.pallas_call(kernel, out_shape=(jax.ShapeDtypeStruct((ROWS, 2, RANK), j...  196 us

profile of v3, /device:TPU:0, one launch (start us, length us, event | category | flops | bytes accessed | tf_op | source)
XLA Modules:
  0.0 199.7 jit_solution(1111256152143009277)
XLA Ops:
  0.6 195.5 %shard_map.50 = (f32[231,2,256]{2,1,0:T(2,128)}, f32[2,32,512]{2,1,0:T(8,128)}) custom-call(bf16[231,2,8192]{2,1,0:T(2,128)(2,1)} %bitcast.4, bf16[231,2,8192]{2,1,0:T(2,128)(2,1)} %bitcast.5, bf16[2,512,256]{2,1,0:T(8,128)(2,1)} %omega.1), custom_call_target="tpu_custom_call" | custom-call | tf_op jit(solution)/shard_map/pallas_call | solution.py:482
  196.1 2.0 copy.7
  198.1 1.6 copy.8

commit v4 on v3

--- a/solution.py
+++ b/solution.py
@@ -125,9 +125,9 @@
     def own(part):
         rows = pl.ds(*CUT_RS[part])
         return (
-            lambda a, b: source.at[pos[0], a, b, rows],
-            lambda a, b: source.at[a, pos[1], b, rows],
-            lambda a, b: source.at[a, b, pos[2], rows],
+            lambda a: source.at[pos[0], a, :, rows],
+            lambda a: source.at[a, pos[1], :, rows],
+            lambda a: source.at[a, :, pos[2], rows],
         )[ORDERS[part][0]]
 
     def second(part, at):
@@ -151,13 +151,12 @@
         arrived(part, 0)
         here, got, held = own(part), bufs[part][0], bufs[part][1]
 
-        @pl.loop(0, 16)
-        def _(n, here=here, got=got, held=held):
-            a, b = lax.div(n, 4), lax.rem(n, 4)
-            value = here(a, b)[...].astype(jnp.float32)
+        @pl.loop(0, 4)
+        def _(a, here=here, got=got, held=held):
+            value = here(a)[...].astype(jnp.float32)
             for step in range(3):
-                value += got[step, a, b].astype(jnp.float32)
-            held[a, b] = value.astype(jnp.bfloat16)
+                value += got[step, a].astype(jnp.float32)
+            held[a] = value.astype(jnp.bfloat16)
 
         launch(part, 1, lambda at, part=part: second(part, at))
     for part in PARTS:
@@ -190,22 +189,34 @@
                     copy.wait_recv()
             done = ORDERS[part][:stage]
             index = tuple(slice(None) if a in done else pos[a] for a in range(3)) + (pl.ds(*CUT_AG[part]),)
-            axis = ORDERS[part][stage]
             copies[part, stage] = []
-            for step in (2, 1, 3):
-                copy = send(
-                    blocks.at[index],
-                    blocks.at[index],
-                    send_sems.at[part, stage, step - 1],
-                    recv_sems.at[part, stage, step - 1],
-                    device_at(moved(pos, axis, step), core),
-                )
-                copy.start()
-                copies[part, stage].append(copy)
+            for step in (2, 1, 3) if stage < 2 else (1, 3):
+                push(part, stage, step, index, step - 1)
+
+    def push(part, stage, step, index, sem):
+        copy = send(
+            blocks.at[index],
+            blocks.at[index],
+            send_sems.at[part, stage, sem],
+            recv_sems.at[part, stage, sem],
+            device_at(moved(pos, ORDERS[part][stage], step), core),
+        )
+        copy.start()
+        copies[part, stage].append(copy)
 
     def finish():
         for part in PARTS:
-            for copy in copies[part, 2]:
+            first, _, axis = ORDERS[part]
+            for arrived in tuple(copies[part, 2]):
+                arrived.wait_recv()
+            for step, half, sem in ((1, 0, 1), (3, 2, 3)):
+                behind = lax.rem(pos[axis] + 4 - step, 4)
+                index = tuple(
+                    behind if a == axis else pl.ds(half, 2) if a == first else slice(None) for a in range(3)
+                ) + (pl.ds(*CUT_AG[part]),)
+                push(part, 2, step, index, sem)
+        for part in PARTS:
+            for copy in copies[part, 2][2:]:
                 copy.wait_recv()
         for started in copies.values():
             for copy in started:
@@ -332,19 +343,17 @@
         send(outgoing.at[n], delta.at[n, core], delta_sems.at[0, n], delta_sems.at[1, n], mate).wait()
     finish_map()
 
-    def swap(part, got, which):
-        copy = send(part, got, swap_sems.at[0, which], swap_sems.at[1, which], mate)
-        copy.start()
-        copy.wait()
-
     def product(right, part, got, which):
         copies = []
         for order, m in enumerate((1 - core, core)):
             part[m] = jnp.zeros((2 * PAD, RANK), jnp.float32)
 
-            @pl.loop(0, 8)
-            def _(i, m=m):
-                part[m] += dot(delta[i, :, m].reshape(2 * PAD, WIDE), right(i, m), 1, 0)
+            @pl.loop(0, 4)
+            def _(n, m=m):
+                two = [
+                    dot(delta[i, :, m].reshape(2 * PAD, WIDE), right(i, m), 1, 0) for i in (2 * n, 2 * n + 1)
+                ]
+                part[m] += two[0] + two[1]
 
             copy = send(part.at[m], got.at[m], swap_sems.at[0, which + order], swap_sems.at[1, which + order], mate)
             copy.start()
@@ -375,9 +384,11 @@
         gram_sum(pos, core, panel[core], pieces, gram_got, gram_mine, gram, gram_sems)
         finish()
         invert_factor(gram, work, factor.at[core])
-        swap(factor.at[core], factor.at[core], which)
-        for m in range(2):
-            turned[m] = dot(factor[m], panel[m], 1, 1, HI).astype(jnp.bfloat16)
+        copy = send(factor.at[core], factor.at[core], swap_sems.at[0, which], swap_sems.at[1, which], mate)
+        copy.start()
+        turned[core] = dot(factor[core], panel[core], 1, 1, HI).astype(jnp.bfloat16)
+        copy.wait()
+        turned[1 - core] = dot(factor[1 - core], panel[1 - core], 1, 1, HI).astype(jnp.bfloat16)
 
     def sketch_rows(i, m):
         x, yh = lax.div(i, 2), lax.rem(i, 2)
@@ -461,8 +472,8 @@
         dma((6, 3, 3)),
         dma((2, 6, 4, 3)),
         pltpu.VMEM((4, 4, 4, SUB, RANK), half),
-        dma((6, 3, 3)),
-        dma((6, 3, 3)),
+        dma((6, 3, 4)),
+        dma((6, 3, 4)),
         pltpu.VMEM((64, 8, SUB), full),
         pltpu.VMEM((64, 8, SUB), full),
         pltpu.VMEM((8, SUB), full),

time: 200 us -> 192 us (0.960)
  Pallas kernels: 196 us -> 188 us
    pallas_call x1, Pallas kernels: 196 us -> 188 us  [local(): pl.pallas_call(kernel, out_shape=(jax.ShapeDtypeStruct((ROWS, 2, RANK), j...]
where the time goes in v4:
time: 192 us
  Pallas kernels  188 us (98%)
  local copies, waits for them, and re-layouts  3.53 us (2%)
    pallas_call x1, Pallas kernels, local(): pl.pallas_call(kernel, out_shape=(jax.ShapeDtypeStruct((ROWS, 2, RANK), j...  188 us

profile of v4, /device:TPU:0, one launch (start us, length us, event | category | flops | bytes accessed | tf_op | source)
XLA Modules:
  0.0 191.9 jit_solution(1735730676186553583)
XLA Ops:
  0.6 187.7 %shard_map.50 = (f32[231,2,256]{2,1,0:T(2,128)}, f32[2,32,512]{2,1,0:T(8,128)}) custom-call(bf16[231,2,8192]{2,1,0:T(2,128)(2,1)} %bitcast.4, bf16[231,2,8192]{2,1,0:T(2,128)(2,1)} %bitcast.5, bf16[2,512,256]{2,1,0:T(8,128)(2,1)} %omega.1), custom_call_target="tpu_custom_call" | custom-call | tf_op jit(solution)/shard_map/pallas_call | solution.py:493
  188.4 2.0 %copy.7 = f32[2,231,256]{2,0,1:T(2,128)} copy(f32[2,231,256]{2,0,1:T(2,128)} %bitcast.6) | data formatting | bytes 946176
  190.3 1.6 copy.8

commit v5 on v4

--- a/solution.py
+++ b/solution.py
@@ -333,12 +333,11 @@
             if leaving:
                 send(outgoing.at[n], delta.at[n, core], delta_sems.at[0, n], delta_sems.at[1, n], mate).start()
 
-    subtract(0, 3, True)
+    subtract(0, 2, True)
     launch_map(1)
-    subtract(3, 8, True)
-    subtract(8, 9, False)
+    subtract(2, 8, True)
     launch_map(2)
-    subtract(9, 16, False)
+    subtract(8, 16, False)
     for n in range(8):
         send(outgoing.at[n], delta.at[n, core], delta_sems.at[0, n], delta_sems.at[1, n], mate).wait()
     finish_map()

time: 192 us -> 191 us (level)
  no operation moved by 1% of the time
where the time goes in v5:
time: 191 us
  Pallas kernels  187 us (98%)
  local copies, waits for them, and re-layouts  3.53 us (2%)
    pallas_call x1, Pallas kernels, local(): pl.pallas_call(kernel, out_shape=(jax.ShapeDtypeStruct((ROWS, 2, RANK), j...  187 us

profile of v5, /device:TPU:0, one launch (start us, length us, event | category | flops | bytes accessed | tf_op | source)
XLA Modules:
  0.0 191.2 jit_solution(10832131090087057225)
XLA Ops:
  0.6 187.1 %shard_map.50 = (f32[231,2,256]{2,1,0:T(2,128)}, f32[2,32,512]{2,1,0:T(8,128)}) custom-call(bf16[231,2,8192]{2,1,0:T(2,128)(2,1)} %bitcast.4, bf16[231,2,8192]{2,1,0:T(2,128)(2,1)} %bitcast.5, bf16[2,512,256]{2,1,0:T(8,128)(2,1)} %omega.1), custom_call_target="tpu_custom_call" | custom-call | tf_op jit(solution)/shard_map/pallas_call | solution.py:492
  187.7 2.0 %copy.7 = f32[2,231,256]{2,0,1:T(2,128)} copy(f32[2,231,256]{2,0,1:T(2,128)} %bitcast.6) | data formatting | bytes 946176
  189.7 1.6 copy.8
